TPU v7x, 32 devices: a whole 2x2x4 slice. The times are simulated.
32 devices in a mesh: groups: 2 (over y), expert: 4 (over z), dp: 2 (over x), inner: 2 (over core).
Axes of the slice: x: 2, y: 2, z: 4, core: 2. Of those that a mesh axis runs over, the one named last changes fastest.
Arguments:
- tokens: bfloat16 [2048, 1536], P(('groups', 'expert', 'dp'), 'inner'), parts along dimension 0, may hold values from -6 to 6
- out_grad: bfloat16 [2048, 1536], P(('groups', 'expert', 'dp'), 'inner'), parts along dimension 0, may hold values from -6 to 6
- expert_ids: int32 [2048, 8], P(('groups', 'expert', 'dp')), parts along dimension 0, may hold values from 0 to 63, all different within a row; in each aligned block of 128 rows (0 to 127, 128 to 255, ...) at most 17 rows name the same one
- gate_probs: float32 [2048, 8], P(('groups', 'expert', 'dp')), parts along dimension 0, may hold values from 0.05 to 0.5
- gate_weight: bfloat16 [64, 1536, 384], P('expert', 'inner', 'dp'), may hold values from -0.15625 to 0.15625
- up_weight: bfloat16 [64, 1536, 384], P('expert', 'inner', 'dp'), may hold values from -0.15625 to 0.15625
- down_weight: bfloat16 [64, 384, 1536], P('expert', 'dp', 'inner'), may hold values from -0.3125 to 0.3125
Outputs:
- token_grad: bfloat16 [2048, 1536], P(('groups', 'expert', 'dp'), 'inner'), parts along dimension 0
- prob_grad: float32 [2048, 8], P(('groups', 'expert', 'dp')), parts along dimension 0
- gate_weight_grad: bfloat16 [128, 1536, 384], P(('groups', 'expert'), 'inner', 'dp'), parts along dimension 0
- up_weight_grad: bfloat16 [128, 1536, 384], P(('groups', 'expert'), 'inner', 'dp'), parts along dimension 0
- down_weight_grad: bfloat16 [128, 384, 1536], P(('groups', 'expert'), 'dp', 'inner'), parts along dimension 0
There are 2 independent parts, one for each index of `groups`. A program takes and returns all parts, laid end to end along the dimension named above; an argument that names none is the same for every part. Nothing has to cross between parts.
Inputs may be any that keep to these rules, and one draw needn't show every extreme that they name: `expert_ids`: within the rows of one block of 128 tokens no expert is chosen more than 17 times, and some expert is chosen exactly 17 times in some block; a token's 8 experts differ.
All inputs are finite; a program needn't handle non-finite values.
Results may differ from a plain program's by a relative error of at most 0.015.
Values may be sent and summed in bfloat16 or wider, within the bound.
A program may use at most 192 MiB of HBM per device.

v0:
```python
import jax
import jax.numpy as jnp
from jax import lax
from jax.sharding import PartitionSpec as P


def on_device(tokens, out_grad, expert_ids, gate_probs, gate_weight, up_weight, down_weight):
    tok_rows, width_half = tokens.shape
    top_count = expert_ids.shape[1]
    per_dev = gate_weight.shape[0]
    owners = lax.axis_size("expert")
    experts = per_dev * owners
    capacity = tok_rows * top_count // experts + 1
    row_count = owners * capacity
    total_slots = experts * capacity
    pair_count = tok_rows * top_count
    chosen = expert_ids.reshape(-1)
    matches = (chosen[:, None] == jnp.arange(experts, dtype=jnp.int32)[None, :]).astype(jnp.int32)
    before = jnp.cumsum(matches, axis=0) - matches
    slot_index = jnp.sum(before * matches, axis=1)
    target = chosen % per_dev * row_count + chosen // per_dev * capacity + slot_index
    source_tok = (
        jnp.zeros((total_slots,), jnp.int32)
        .at[target]
        .set(jnp.arange(pair_count, dtype=jnp.int32) // top_count)
    )
    filled = jnp.zeros((total_slots,), jnp.bfloat16).at[target].set(1)
    slot_probs = (
        jnp.zeros((total_slots,), jnp.float32)
        .at[target]
        .set(gate_probs.reshape(-1))
        .astype(jnp.bfloat16)
    )
    sent_rows = (tokens[source_tok] * filled[:, None]).reshape(
        per_dev, owners, capacity, width_half
    )
    sent_grads = (out_grad[source_tok] * filled[:, None]).reshape(
        per_dev, owners, capacity, width_half
    )
    sent_probs = slot_probs.reshape(per_dev, owners, capacity)
    arrived_rows, arrived_grads, arrived_probs = (
        lax.all_to_all(sent_rows, "expert", split_axis=1, concat_axis=1, tiled=True),
        lax.all_to_all(sent_grads, "expert", split_axis=1, concat_axis=1, tiled=True),
        lax.all_to_all(sent_probs, "expert", split_axis=1, concat_axis=1, tiled=True),
    )
    full_gate, full_up, full_down = (
        lax.all_gather(gate_weight, "dp", axis=2, tiled=True),
        lax.all_gather(up_weight, "dp", axis=2, tiled=True),
        lax.all_gather(down_weight, "dp", axis=1, tiled=True),
    )
    expert_rows = arrived_rows.reshape(per_dev, row_count, width_half)
    gate_part = jnp.einsum(
        "jrd,jdf->jrf", expert_rows, full_gate, preferred_element_type=jnp.float32
    )
    up_part = jnp.einsum("jrd,jdf->jrf", expert_rows, full_up, preferred_element_type=jnp.float32)
    gate_sum, up_sum = (
        lax.psum(gate_part.astype(jnp.bfloat16), "inner").astype(jnp.float32),
        lax.psum(up_part.astype(jnp.bfloat16), "inner").astype(jnp.float32),
    )
    sigmoid_gate = jax.nn.sigmoid(gate_sum)
    activated = gate_sum * sigmoid_gate
    hidden = (activated * up_sum).astype(jnp.bfloat16)
    expert_grads = arrived_grads.reshape(per_dev, row_count, width_half)
    prob_col = arrived_probs.reshape(per_dev, row_count, 1).astype(jnp.float32)
    slope_part = jnp.einsum(
        "jrd,jfd->jrf", expert_grads, full_down, preferred_element_type=jnp.float32
    )
    slope_sum = lax.psum(slope_part.astype(jnp.bfloat16), "inner").astype(jnp.float32)
    scores = jnp.sum(hidden.astype(jnp.float32) * slope_sum, axis=-1)
    hidden_grad = prob_col * slope_sum
    gate_back = (
        hidden_grad * up_sum * sigmoid_gate * (1.0 + gate_sum * (1.0 - sigmoid_gate))
    ).astype(jnp.bfloat16)
    up_back = (hidden_grad * activated).astype(jnp.bfloat16)
    row_grads = jnp.einsum("jrf,jdf->jrd", gate_back, full_gate, preferred_element_type=jnp.float32)
    row_grads = (
        row_grads + jnp.einsum("jrf,jdf->jrd", up_back, full_up, preferred_element_type=jnp.float32)
    ).astype(jnp.bfloat16)
    returned_rows, returned_scores = (
        lax.all_to_all(
            row_grads.reshape(per_dev, owners, capacity, width_half),
            "expert",
            split_axis=1,
            concat_axis=1,
            tiled=True,
        ),
        lax.all_to_all(
            scores.astype(jnp.bfloat16).reshape(per_dev, owners, capacity),
            "expert",
            split_axis=1,
            concat_axis=1,
            tiled=True,
        ),
    )
    pair_rows = returned_rows.reshape(total_slots, width_half)[target]
    token_grad = jnp.sum(
        pair_rows.reshape(tok_rows, top_count, width_half).astype(jnp.float32), axis=1
    ).astype(jnp.bfloat16)
    prob_grad = returned_scores.reshape(-1)[target].astype(jnp.float32).reshape(tok_rows, top_count)
    grad_gate = jnp.einsum(
        "jrd,jrf->jdf", expert_rows, gate_back, preferred_element_type=jnp.float32
    )
    grad_up = jnp.einsum("jrd,jrf->jdf", expert_rows, up_back, preferred_element_type=jnp.float32)
    down_rows = (prob_col * expert_grads).astype(jnp.bfloat16)
    grad_down = jnp.einsum("jrf,jrd->jfd", hidden, down_rows, preferred_element_type=jnp.float32)
    summed_gate, summed_up, summed_down = (
        lax.psum_scatter(
            grad_gate.astype(jnp.bfloat16), "dp", scatter_dimension=2, tiled=True
        ).astype(jnp.float32),
        lax.psum_scatter(
            grad_up.astype(jnp.bfloat16), "dp", scatter_dimension=2, tiled=True
        ).astype(jnp.float32),
        lax.psum_scatter(
            grad_down.astype(jnp.bfloat16), "dp", scatter_dimension=1, tiled=True
        ).astype(jnp.float32),
    )
    return (
        token_grad,
        prob_grad,
        summed_gate.astype(jnp.bfloat16),
        summed_up.astype(jnp.bfloat16),
        summed_down.astype(jnp.bfloat16),
    )


def solution(mesh):
    placed = (
        P(("groups", "expert", "dp"), "inner"),
        P(("groups", "expert", "dp"), "inner"),
        P(("groups", "expert", "dp"), None),
        P(("groups", "expert", "dp"), None),
        P("expert", "inner", "dp"),
        P("expert", "inner", "dp"),
        P("expert", "dp", "inner"),
    )
    return jax.shard_map(
        on_device,
        mesh=mesh,
        in_specs=placed,
        out_specs=(
            P(("groups", "expert", "dp"), "inner"),
            P(("groups", "expert", "dp"), None),
            P(("groups", "expert"), "inner", "dp"),
            P(("groups", "expert"), "inner", "dp"),
            P(("groups", "expert"), "dp", "inner"),
        ),
        check_vma=False,
    )
```

profile of v0, /device:TPU:0, one launch (start us, length us, event | category | flops | bytes accessed | tf_op | source)
XLA Modules:
  0.0 753.5 jit_solution(1835674188766818200)
XLA Ops:
  7.2 0.7 all-gather.6.cloned.1.call-update
  8.0 0.7 all-gather.8.cloned.1.call-update
  8.7 0.7 all-gather.4.cloned.1.call-update
  9.4 0.1 copy.48
  9.5 0.1 eq.31
  9.7 0.1 reshape.205
  9.8 18.0 %reduce-window.6 = s32[64,8,128]{2,1,0:T(8,128)S(1)} reduce-window(s32[64,8,128]{2,1,0:T(8,128)S(1)} %fusion.24, s32[]{:T(128)} %constant.51.clone.1), window={size=1x1x128 pad=0_0x0_0x127_0}, to_apply=%region_0.0 | reduce-window | flops 8323072 | bytes 524292 | tf_op jit(solution)/shard_map/reduce-window
  27.8 0.1 slice.16
  28.0 0.1 copy.51
  28.3 0.1 broadcast_add_fusion
  28.5 4.3 scatter_custom_fusion.1
  32.9 4.8 gather_fusion.1
  37.7 2.5 gather.19
  40.2 7.6 %scatter_custom_fusion.2 = bf16[1088]{0:T(1024)(128)(2,1)S(1)} fusion(s32[1024]{0:T(1024)S(1)} %bitcast.54, bf16[1024]{0:T(1024)(128)(2,1)S(1)} %broadcast.149, bf16[]{:T(256)} %constant.63.clone.1), kind=kCustom, calls=%fused_computation.74 | custom fusion | bytes 2178 | tf_op jit(solution)/shard_map/scatter | solution.py:27
  47.8 0.1 mul.93
  48.0 4.8 gather_fusion
  52.8 3.6 gather.17
  56.4 3.4 broadcast_multiply_fusion
  59.8 2.1 copy.58
  61.9 6.3 all-to-all-start.2
  68.3 3.8 copy.56
  72.1 35.3 %all-to-all-done.2 = bf16[16,4,17,768]{3,0,2,1:T(8,128)(2,1)S(1)} async-done(((bf16[16,4,17,768]{3,0,2,1:T(8,128)(2,1)}), bf16[16,4,17,768]{3,0,2,1:T(8,128)(2,1)S(1)}, u32[]{:S(2)}, u32[]{:S(2)}) %all-to-all-start.2) | async-done | bytes 1671200 | tf_op jit(solution)/shard_map/all_to_all | solution.py:42
  107.3 3.6 all-to-all-start.1
  110.9 0.5 all-reduce.3.cloned.1.call-start
  111.4 18.8 %all-gather.6.cloned.1.call-done = bf16[16,768,384]{1,2,0:T(8,128)(2,1)} async-done(((bf16[16,768,192]{1,2,0:T(8,128)(2,1)}), bf16[16,768,384]{1,2,0:T(8,128)(2,1)}) %all-gather.6.cloned.1.call-update) | async-done | bytes 9437200 | tf_op jit(solution)/shard_map/all_gather | solution.py:48
  130.2 7.4 convolution_convert_fusion.4
  137.7 112.2 %all-gather.8.cloned.1.call-done = bf16[16,768,384]{1,2,0:T(8,128)(2,1)} async-done(((bf16[16,768,192]{1,2,0:T(8,128)(2,1)}), bf16[16,768,384]{1,2,0:T(8,128)(2,1)}) %all-gather.8.cloned.1.call-update) | async-done | bytes 9437200 | tf_op jit(solution)/shard_map/all_gather | solution.py:47
  249.8 7.5 convolution_convert_fusion.3
  257.3 112.0 %all-gather.4.cloned.1.call-done = bf16[16,384,768]{2,1,0:T(8,128)(2,1)} async-done(((bf16[16,192,768]{2,1,0:T(8,128)(2,1)}), bf16[16,384,768]{2,1,0:T(8,128)(2,1)}) %all-gather.4.cloned.1.call-update) | async-done | bytes 9437200 | tf_op jit(solution)/shard_map/all_gather | solution.py:49
  369.3 7.5 fusion.14
  376.9 0.6 copy-done.6
  377.5 0.1 copy.53
  377.7 4.3 scatter_custom_fusion
  382.0 0.1 reshape.208
  382.2 0.1 reshape.281
  382.3 10.0 %all_to_all.25 = bf16[4,2,136]{2,1,0:T(2,128)(2,1)S(1)} all-to-all(bf16[4,2,136]{2,1,0:T(2,128)(2,1)S(1)} %reshape.281), channel_id=1, replica_groups=mesh['groups'=2,'expert'=4,'dp'=2,'inner'=2] {'expert'}, dimensions={0} | all-to-all | bytes 4352 | tf_op jit(solution)/shard_map/all_to_all | solution.py:44
  392.5 7.0 all-reduce.3.cloned.1.call-done
  399.5 8.3 %convolution_convert_fusion.2 = bf16[16,768,384]{1,2,0:T(8,128)(2,1)} fusion(bf16[16,68,768]{2,0,1:T(8,128)(2,1)S(1)} %bitcast.41, bf16[16,68,384]{2,1,0:T(8,128)(2,1)} %get-tuple-element.21, bf16[16,68,384]{2,1,0:T(8,128)(2,1)} %get-tuple-element.20, bf16[16,68,384]{2,1,0:T(8,128)(2,1)} %get-tuple-element.22, f32[16,68]{1,0:T(8,128)S(1)} %reshape.215), kind=kOutput, calls=%fused_computation.9 | convolution fusion | flops 652296192 | bytes 13619456 | tf_op jit(solution)/shard_map/jrd,jrf->jdf/dot_general | solution.py:100
  407.8 0.2 reduce-scatter.6.cloned.1.call-start
  408.0 8.2 %convolution_convert_fusion.1 = bf16[16,768,384]{1,2,0:T(8,128)(2,1)} fusion(bf16[16,68,768]{2,0,1:T(8,128)(2,1)S(1)} %bitcast.42, bf16[16,68,384]{2,1,0:T(8,128)(2,1)} %get-tuple-element.20, f32[16,68]{1,0:T(8,128)S(1)} %reshape.215, bf16[16,68,384]{2,1,0:T(8,128)(2,1)} %get-tuple-element.22), kind=kOutput, calls=%fused_computation.8 | convolution fusion | flops 650207232 | bytes 12783872 | tf_op jit(solution)/shard_map/jrd,jrf->jdf/dot_general | solution.py:103
  416.3 0.1 copy.67
  416.4 0.4 multiply_convert_fusion
  416.8 0.7 copy-done.4
  417.4 7.6 %convolution_convert_fusion = bf16[16,384,768]{2,1,0:T(8,128)(2,1)} fusion(bf16[16,68,768]{2,0,1:T(8,128)(2,1)S(1)} %multiply_convert_fusion, bf16[16,68,384]{2,1,0:T(8,128)(2,1)} %get-tuple-element.21, bf16[16,68,384]{2,1,0:T(8,128)(2,1)S(1)} %copy-done.4), kind=kOutput, calls=%fused_computation.7 | convolution fusion | flops 649789440 | bytes 12779520 | tf_op jit(solution)/shard_map/jrf,jrd->jfd/dot_general | solution.py:105
  425.0 1.2 copy-done.3
  426.2 2.1 fusion.2
  428.3 0.7 reshape.283
  429.0 4.8 all-to-all-start.4
  433.9 6.1 fusion.41
  440.0 0.6 slice-done.2
  440.6 2.0 add_convert_fusion
  442.6 1.5 copy.61
  444.1 5.3 all-to-all-start.3
  449.5 0.1 reshape.214
  449.7 6.8 gather_fusion.3
  456.6 0.7 copy.69
  457.2 31.1 %all-to-all-done.3 = bf16[16,4,17,768]{3,0,2,1:T(8,128)(2,1)S(1)} async-done(((bf16[16,4,17,768]{3,0,2,1:T(8,128)(2,1)}), bf16[16,4,17,768]{3,0,2,1:T(8,128)(2,1)S(1)}, u32[]{:S(2)}, u32[]{:S(2)}) %all-to-all-start.3) | async-done | bytes 1671200 | tf_op jit(solution)/shard_map/all_to_all | solution.py:80
  488.3 2.1 copy.62
  490.4 2.7 reshape.212
  493.1 4.0 gather_fusion.2
  497.1 1.7 bitcast_reduce_fusion
  498.8 20.8 %reduce-scatter.4.cloned.1.call-done = bf16[16,768,192]{1,2,0:T(8,128)(2,1)} async-done(((bf16[16,768,384]{1,2,0:T(8,128)(2,1)}), bf16[16,768,192]{1,2,0:T(8,128)(2,1)}) %reduce-scatter.4.cloned.1.call-update) | async-done | bytes 4718608 | tf_op jit(solution)/shard_map/reduce_scatter | solution.py:107
  519.6 113.3 %reduce-scatter.6.cloned.1.call-done = bf16[16,768,192]{1,2,0:T(8,128)(2,1)} async-done(((bf16[16,768,384]{1,2,0:T(8,128)(2,1)}), bf16[16,768,192]{1,2,0:T(8,128)(2,1)}) %reduce-scatter.6.cloned.1.call-update) | async-done | bytes 4718608 | tf_op jit(solution)/shard_map/reduce_scatter | solution.py:110
  633.0 113.5 %reduce-scatter.8.cloned.1.call-done = bf16[16,192,768]{2,1,0:T(8,128)(2,1)} async-done(((bf16[16,384,768]{2,1,0:T(8,128)(2,1)}), bf16[16,192,768]{2,1,0:T(8,128)(2,1)}) %reduce-scatter.8.cloned.1.call-update) | async-done | bytes 4718608 | tf_op jit(solution)/shard_map/reduce_scatter | solution.py:113
  (51 shorter events, 1.2 us)
Async XLA Ops:
  7.2 25.7 %copy-start = (bf16[128,768]{1,0:T(8,128)(2,1)S(1)}, bf16[128,768]{1,0:T(8,128)(2,1)}, u32[]{:S(2)}) copy-start(bf16[128,768]{1,0:T(8,128)(2,1)} %param.7) | copy-start | bytes 589828
  7.2 123.1 %all-gather.6.cloned.1.call-start = ((), (), s32[]{:S(2)}) async-start(), calls=%async_computation.9 | async-start | bytes 14155776 | tf_op jit(solution)/shard_map/all_gather | solution.py:48
  7.9 241.9 %all-gather.8.cloned.1.call-start = ((), (), s32[]{:S(2)}) async-start(), calls=%async_computation.10 | async-start | bytes 14155776 | tf_op jit(solution)/shard_map/all_gather | solution.py:47
  8.7 0.7 copy-start.5
  8.7 360.6 %all-gather.4.cloned.1.call-start = ((), (), s32[]{:S(2)}) async-start(), calls=%async_computation.8 | async-start | bytes 14155776 | tf_op jit(solution)/shard_map/all_gather | solution.py:49
  37.7 10.3 %copy-start.2 = (bf16[128,768]{1,0:T(8,128)(2,1)S(1)}, bf16[128,768]{1,0:T(8,128)(2,1)}, u32[]{:S(2)}) copy-start(bf16[128,768]{1,0:T(8,128)(2,1)} %param.8) | copy-start | bytes 589828
  61.9 45.4 %all-to-all-start.2 = ((bf16[16,4,17,768]{3,0,2,1:T(8,128)(2,1)}), bf16[16,4,17,768]{3,0,2,1:T(8,128)(2,1)S(1)}, u32[]{:S(2)}, u32[]{:S(2)}) async-start(bf16[16,4,17,768]{3,0,2,1:T(8,128)(2,1)} %copy.58), calls=%async_computation.2 | async-start | bytes 3342336 | tf_op jit(solution)/shard_map/all_to_all | solution.py:42
  107.3 150.0 %all-to-all-start.1 = ((bf16[16,4,17,768]{3,0,2,1:T(8,128)(2,1)}), bf16[16,4,17,768]{3,0,2,1:T(8,128)(2,1)S(1)}, u32[]{:S(2)}, u32[]{:S(2)}) async-start(bf16[16,4,17,768]{3,0,2,1:T(8,128)(2,1)} %copy.56), calls=%async_computation.1 | async-start | bytes 3342336 | tf_op jit(solution)/shard_map/all_to_all | solution.py:43
  110.9 288.5 %all-reduce.3.cloned.1.call-start = ((), (), s32[]{:S(2)}) async-start(), calls=%async_computation.14 | async-start | bytes 5308416 | tf_op jit(solution)/shard_map/psum | solution.py:68
  376.8 0.7 copy-start.6
  376.8 142.8 %reduce-scatter.4.cloned.1.call-start = ((), (), s32[]{:S(2)}) async-start(), calls=%async_computation.11 | async-start | bytes 14155776 | tf_op jit(solution)/shard_map/reduce_scatter | solution.py:107
  407.8 225.2 %reduce-scatter.6.cloned.1.call-start = ((), (), s32[]{:S(2)}) async-start(), calls=%async_computation.12 | async-start | bytes 14155776 | tf_op jit(solution)/shard_map/reduce_scatter | solution.py:110
  416.2 1.2 copy-start.4
  416.2 330.2 %reduce-scatter.8.cloned.1.call-start = ((), (), s32[]{:S(2)}) async-start(), calls=%async_computation.13 | async-start | bytes 14155776 | tf_op jit(solution)/shard_map/reduce_scatter | solution.py:113
  425.0 1.2 copy-start.3
  426.2 13.8 %slice-start = ((s8[9437184]{0:T(1024)(128)(4,1)}), s8[1048576]{0:T(1024)(128)(4,1)S(1)}, s32[]{:S(2)}) async-start(s8[9437184]{0:T(1024)(128)(4,1)} %bitcast.44), calls=%async_computation.15 | async-start | bytes 2097152
  429.0 15.0 %all-to-all-start.4 = ((bf16[4,2,136]{2,1,0:T(2,128)(2,1)}), bf16[4,2,136]{2,1,0:T(2,128)(2,1)S(1)}, u32[]{:S(2)}, u32[]{:S(2)}) async-start(bf16[4,2,136]{2,1,0:T(2,128)(2,1)} %reshape.283), calls=%async_computation.4 | async-start | bytes 8192 | tf_op jit(solution)/shard_map/all_to_all | solution.py:87
  433.9 6.1 slice-start.1
  433.9 6.7 slice-start.2
  444.1 44.2 %all-to-all-start.3 = ((bf16[16,4,17,768]{3,0,2,1:T(8,128)(2,1)}), bf16[16,4,17,768]{3,0,2,1:T(8,128)(2,1)S(1)}, u32[]{:S(2)}, u32[]{:S(2)}) async-start(bf16[16,4,17,768]{3,0,2,1:T(8,128)(2,1)} %bitcast.6), calls=%async_computation.3 | async-start | bytes 3342336 | tf_op jit(solution)/shard_map/all_to_all | solution.py:80
  493.1 253.4 %copy-start.1 = (bf16[128,768]{1,0:T(8,128)(2,1)S(1)}, bf16[128,768]{1,0:T(8,128)(2,1)}, u32[]{:S(2)}) copy-start(bf16[128,768]{1,0:T(8,128)(2,1)} %param.7) | copy-start | bytes 589828
Sparse Core Ops, SparseCore 0:
  9.6 120.6 all-gather.5
  131.8 117.9 all-gather.7
  251.4 117.8 all-gather.3
  376.9 22.4 all-reduce.2
  407.9 111.6 reduce-scatter.3
  522.4 110.5 reduce-scatter.5
  635.9 110.5 reduce-scatter.7
where the time goes:
time: 762 us; the launch traced here: 754 us
  waiting for transfers between devices  566 us (74%)
  local copies, waits for them, and re-layouts  61.4 us (8%)
  matrix products  54.5 us (7%)
  other arithmetic  25.9 us (3%)
  starting transfers between devices  20.9 us (3%)
  between operations  14.7 us (2%)
  blocking collectives  10 us (1%)
    reduce_scatter x1, waiting for transfers between devices, on_device(): lax.psum_scatter(grad_down.astype(jnp.bfloat16), 'dp', scatter_dimension=...  113 us
    reduce_scatter x1, waiting for transfers between devices, on_device(): lax.psum_scatter(grad_up.astype(jnp.bfloat16), 'dp', scatter_dimension=2,...  113 us
    all_gather x1, waiting for transfers between devices, on_device(): lax.all_gather(gate_weight, 'dp', axis=2, tiled=True)  112 us
    all_gather x1, waiting for transfers between devices, on_device(): lax.all_gather(down_weight, 'dp', axis=1, tiled=True)  112 us
    all_to_all x1, waiting for transfers between devices, on_device(): lax.all_to_all(sent_rows, 'expert', split_axis=1, concat_axis=1, tiled=True)  35.3 us
    all_to_all x1, waiting for transfers between devices, on_device(): lax.all_to_all(row_grads.reshape(per_dev, owners, capacity, width_half),...  31.1 us
    reduce_scatter x1, waiting for transfers between devices, on_device(): lax.psum_scatter(grad_gate.astype(jnp.bfloat16), 'dp', scatter_dimension=...  20.8 us
    all_gather x1, waiting for transfers between devices, on_device(): lax.all_gather(up_weight, 'dp', axis=2, tiled=True)  18.8 us
  transfers between devices with their start and end apart: 11, of which 9 were waited for; matrix products, arithmetic and copies ran while one was open for 16% of the time, Pallas kernels for 0%

commit v1 on v0

--- a/solution.py
+++ b/solution.py
@@ -2,6 +2,18 @@
 import jax.numpy as jnp
 from jax import lax
 from jax.sharding import PartitionSpec as P
+
+
+def gather_by_bits(shard, axis, dim):
+    ways, here = (lax.axis_size(axis), lax.axis_index(axis))
+    grown, reach = (shard, 1)
+    while reach < ways:
+        theirs = lax.ppermute(grown, axis, [(d, d ^ reach) for d in range(ways)])
+        mine_first = jnp.concatenate([grown, theirs], axis=dim)
+        theirs_first = jnp.concatenate([theirs, grown], axis=dim)
+        grown = jnp.where(here & reach == 0, mine_first, theirs_first)
+        reach = 2 * reach
+    return grown
 
 
 def on_device(tokens, out_grad, expert_ids, gate_probs, gate_weight, up_weight, down_weight):
@@ -44,7 +56,7 @@
         lax.all_to_all(sent_probs, "expert", split_axis=1, concat_axis=1, tiled=True),
     )
     full_gate, full_up, full_down = (
-        lax.all_gather(gate_weight, "dp", axis=2, tiled=True),
+        gather_by_bits(gate_weight, "dp", 2),
         lax.all_gather(up_weight, "dp", axis=2, tiled=True),
         lax.all_gather(down_weight, "dp", axis=1, tiled=True),
     )

time: 762 us -> 729 us (0.957)
  waiting for transfers between devices: 566 us -> 521 us
  matrix products: 54.5 us -> 67.3 us
    all_gather x1 -> x0, waiting for transfers between devices: 112 us -> none  [on_device(): lax.all_gather(gate_weight, 'dp', axis=2, tiled=True)]
    ppermute x0 -> x1, waiting for transfers between devices: none -> 88.3 us  [gather_by_bits(): theirs = lax.ppermute(grown, axis, [(d, d ^ reach) for d in range(ways)])]
    all_gather x1, waiting for transfers between devices: 18.8 us -> 4.68 us  [on_device(): lax.all_gather(up_weight, 'dp', axis=2, tiled=True)]
    reduce_scatter x1, waiting for transfers between devices: 20.8 us -> 12.1 us  [on_device(): lax.psum_scatter(grad_gate.astype(jnp.bfloat16), 'dp', scatter_dimension=...]
  transfers between devices with their start and end apart: 11 -> 11, of which waited for: 9 -> 9; matrix products, arithmetic and copies ran while one was open for 16% -> 19% of each run, Pallas kernels for 0% -> 0%
where the time goes in v1:
time: 729 us; the launch traced here: 720 us
  waiting for transfers between devices  521 us (71%)
  matrix products  67.3 us (9%)
  local copies, waits for them, and re-layouts  59.1 us (8%)
  other arithmetic  25.8 us (4%)
  starting transfers between devices  22.7 us (3%)
  between operations  14.6 us (2%)
  blocking collectives  9.97 us (1%)
    reduce_scatter x1, waiting for transfers between devices, on_device(): lax.psum_scatter(grad_up.astype(jnp.bfloat16), 'dp', scatter_dimension=2,...  113 us
    reduce_scatter x1, waiting for transfers between devices, on_device(): lax.psum_scatter(grad_down.astype(jnp.bfloat16), 'dp', scatter_dimension=...  113 us
    all_gather x1, waiting for transfers between devices, on_device(): lax.all_gather(down_weight, 'dp', axis=1, tiled=True)  113 us
    ppermute x1, waiting for transfers between devices, gather_by_bits(): theirs = lax.ppermute(grown, axis, [(d, d ^ reach) for d in range(ways)])  88.3 us
    all_to_all x1, waiting for transfers between devices, on_device(): lax.all_to_all(sent_rows, 'expert', split_axis=1, concat_axis=1, tiled=True)  36.7 us
    all_to_all x1, waiting for transfers between devices, on_device(): lax.all_to_all(row_grads.reshape(per_dev, owners, capacity, width_half),...  31.1 us
    another operation x3, other arithmetic  18.2 us
  transfers between devices with their start and end apart: 11, of which 9 were waited for; matrix products, arithmetic and copies ran while one was open for 19% of the time, Pallas kernels for 0%

profile of v1, /device:TPU:0, one launch (start us, length us, event | category | flops | bytes accessed | tf_op | source)
XLA Modules:
  0.0 720.5 jit_solution(17001487226899987799)
XLA Ops:
  7.2 0.7 all-gather.5.cloned.1.call-update
  8.0 0.7 all-gather.3.cloned.1.call-update
  8.7 3.0 collective-permute-start
  11.7 0.1 copy.54
  11.8 0.1 eq.34
  12.0 0.1 reshape.205
  12.1 18.0 %reduce-window.6 = s32[64,8,128]{2,1,0:T(8,128)S(1)} reduce-window(s32[64,8,128]{2,1,0:T(8,128)S(1)} %fusion.26, s32[]{:T(128)} %constant.55.clone.1), window={size=1x1x128 pad=0_0x0_0x127_0}, to_apply=%region_0.0 | reduce-window | flops 8323072 | bytes 524292 | tf_op jit(solution)/shard_map/reduce-window
  30.1 0.1 slice.16
  30.2 0.1 copy.57
  30.5 0.1 broadcast_add_fusion
  30.8 4.3 scatter_custom_fusion.1
  35.1 4.8 gather_fusion.1
  39.9 2.5 gather.19
  42.5 7.6 %scatter_custom_fusion.2 = bf16[1088]{0:T(1024)(128)(2,1)S(1)} fusion(s32[1024]{0:T(1024)S(1)} %bitcast.46, bf16[1024]{0:T(1024)(128)(2,1)S(1)} %broadcast.155, bf16[]{:T(256)} %constant.67.clone.1), kind=kCustom, calls=%fused_computation.76 | custom fusion | bytes 2178 | tf_op jit(solution)/shard_map/scatter | solution.py:39
  50.1 0.1 mul.93
  50.2 4.8 gather_fusion
  55.0 3.6 gather.17
  58.6 3.4 broadcast_multiply_fusion
  62.1 2.1 copy.64
  64.2 5.0 all-to-all-start.2
  69.2 2.1 copy.62
  71.4 36.7 %all-to-all-done.2 = bf16[16,4,17,768]{3,0,2,1:T(8,128)(2,1)} async-done(((bf16[16,4,17,768]{3,0,2,1:T(8,128)(2,1)}), bf16[16,4,17,768]{3,0,2,1:T(8,128)(2,1)}, u32[]{:S(2)}, u32[]{:S(2)}) %all-to-all-start.2) | async-done | bytes 1671200 | tf_op jit(solution)/shard_map/all_to_all | solution.py:54
  108.1 3.6 all-to-all-start.1
  111.7 0.3 all-reduce.3.cloned.1.call-start
  112.0 88.3 %collective-permute-done = bf16[16,768,192]{1,2,0:T(8,128)(2,1)} collective-permute-done((bf16[16,768,192]{1,2,0:T(8,128)(2,1)}, bf16[16,768,192]{1,2,0:T(8,128)(2,1)}, u32[]{:S(2)}, u32[]{:S(2)}) %collective-permute-start) | collective-permute-done | bytes 4718624 | tf_op jit(solution)/shard_map/ppermute | solution.py:11
  200.3 10.1 %fusion.18 = bf16[16,68,384]{2,1,0:T(8,128)(2,1)} fusion(bf16[16,768,192]{1,2,0:T(8,128)(2,1)} %collective-permute-done, bf16[16,768,192]{1,2,0:T(8,128)(2,1)} %param.11, pred[]{:T(512)S(6)} %eq.38, bf16[16,68,768]{2,0,1:T(8,128)(2,1)} %bitcast.5), kind=kOutput, calls=%fused_computation.38 | convolution fusion | flops 684613632 | bytes 11943937 | tf_op jit(solution)/shard_map/jrd,jdf->jrf/dot_general | solution.py:64
  210.4 4.7 all-gather.5.cloned.1.call-done
  215.1 8.0 %convolution_convert_fusion.3 = bf16[16,68,384]{2,1,0:T(8,128)(2,1)} fusion(bf16[16,768,384]{1,2,0:T(8,128)(2,1)} %all-gather.5.cloned.1.call-done, bf16[16,68,768]{2,0,1:T(8,128)(2,1)} %bitcast.5), kind=kOutput, calls=%fused_computation.37 | convolution fusion | flops 642146304 | bytes 11943936 | tf_op jit(solution)/shard_map/jrd,jdf->jrf/dot_general | solution.py:67
  223.0 113.0 %all-gather.3.cloned.1.call-done = bf16[16,384,768]{2,1,0:T(8,128)(2,1)} async-done(((bf16[16,192,768]{2,1,0:T(8,128)(2,1)}), bf16[16,384,768]{2,1,0:T(8,128)(2,1)}) %all-gather.3.cloned.1.call-update) | async-done | bytes 9437200 | tf_op jit(solution)/shard_map/all_gather | solution.py:61
  336.1 7.4 %fusion.15 = bf16[16,68,384]{2,1,0:T(8,128)(2,1)} fusion(bf16[16,384,768]{2,1,0:T(8,128)(2,1)} %all-gather.3.cloned.1.call-done, bf16[16,68,768]{2,0,1:T(8,128)(2,1)S(1)} %bitcast.37), kind=kOutput, calls=%fused_computation.36 | convolution fusion | flops 642146304 | bytes 11943936 | tf_op jit(solution)/shard_map/jrd,jfd->jrf/dot_general | solution.py:77
  343.6 0.6 copy-done.8
  344.2 0.1 copy.59
  344.3 0.1 reshape.253
  344.4 4.3 scatter_custom_fusion
  348.7 0.1 reshape.208
  348.9 0.1 reshape.281
  349.0 10.0 %all_to_all.25 = bf16[4,2,136]{2,1,0:T(2,128)(2,1)S(1)} all-to-all(bf16[4,2,136]{2,1,0:T(2,128)(2,1)S(1)} %reshape.281), channel_id=1, replica_groups=mesh['groups'=2,'expert'=4,'dp'=2,'inner'=2] {'expert'}, dimensions={0} | all-to-all | bytes 4352 | tf_op jit(solution)/shard_map/all_to_all | solution.py:56
  359.2 7.0 all-reduce.3.cloned.1.call-done
  366.1 8.8 %convolution_convert_fusion.2 = bf16[16,768,384]{1,2,0:T(8,128)(2,1)} fusion(bf16[16,68,768]{2,0,1:T(8,128)(2,1)} %bitcast.5, bf16[16,68,384]{2,1,0:T(8,128)(2,1)} %get-tuple-element.21, bf16[16,68,384]{2,1,0:T(8,128)(2,1)} %get-tuple-element.20, bf16[16,68,384]{2,1,0:T(8,128)(2,1)} %get-tuple-element.22, f32[16,68]{1,0:T(8,128)S(1)} %reshape.215), kind=kOutput, calls=%fused_computation.10 | convolution fusion | flops 652296192 | bytes 13619456 | tf_op jit(solution)/shard_map/jrd,jrf->jdf/dot_general | solution.py:112
  374.9 0.5 reduce-scatter.6.cloned.1.call-start
  375.4 0.6 copy-done.4
  376.1 8.4 %convolution_convert_fusion.1 = bf16[16,768,384]{1,2,0:T(8,128)(2,1)} fusion(bf16[16,68,768]{2,0,1:T(8,128)(2,1)} %bitcast.5, bf16[16,68,384]{2,1,0:T(8,128)(2,1)S(1)} %copy-done.4, f32[16,68]{1,0:T(8,128)S(1)} %reshape.215, bf16[16,68,384]{2,1,0:T(8,128)(2,1)} %get-tuple-element.22), kind=kOutput, calls=%fused_computation.9 | convolution fusion | flops 650207232 | bytes 12783872 | tf_op jit(solution)/shard_map/jrd,jrf->jdf/dot_general | solution.py:115
  384.6 0.1 copy.75
  384.7 0.4 multiply_convert_fusion
  385.0 7.9 %convolution_convert_fusion = bf16[16,384,768]{2,1,0:T(8,128)(2,1)} fusion(bf16[16,68,768]{2,0,1:T(8,128)(2,1)S(1)} %multiply_convert_fusion, bf16[16,68,384]{2,1,0:T(8,128)(2,1)} %get-tuple-element.21, bf16[16,68,384]{2,1,0:T(8,128)(2,1)} %get-tuple-element.22), kind=kOutput, calls=%fused_computation.8 | convolution fusion | flops 649789440 | bytes 12779520 | tf_op jit(solution)/shard_map/jrf,jrd->jfd/dot_general | solution.py:117
  392.9 1.2 copy-done.5
  394.1 2.0 fusion.2
  396.1 0.7 reshape.283
  396.8 4.8 all-to-all-start.4
  401.7 6.2 fusion.43
  407.8 10.5 %add_convert_fusion = bf16[16,68,768]{2,1,0:T(8,128)(2,1)S(1)} fusion(f32[16,68,768]{2,1,0:T(8,128)S(1)} %fusion.43, bf16[16,768,192]{1,2,0:T(8,128)(2,1)} %collective-permute-done, bf16[16,768,192]{1,2,0:T(8,128)(2,1)} %param.11, pred[]{:T(512)S(6)} %eq.38, bf16[16,68,384]{2,1,0:T(8,128)(2,1)S(1)} %copy-done.5, bf16[16,68,384]{2,1,0:T(8,128)(2,1)S(1)} %copy-done.4, ...), kind=kOutput, calls=%fused_computation.11 | convolution fusion | flops 691716096 | bytes 16961792 | tf_op jit(solution)/shard_map/jrf,jdf->jrd/dot_general | solution.py:87
  418.4 1.5 copy.69
  419.9 5.3 all-to-all-start.3
  425.3 0.1 reshape.214
  425.5 6.8 gather_fusion.3
  432.4 0.7 copy.77
  433.0 31.1 %all-to-all-done.3 = bf16[16,4,17,768]{3,0,2,1:T(8,128)(2,1)S(1)} async-done(((bf16[16,4,17,768]{3,0,2,1:T(8,128)(2,1)}), bf16[16,4,17,768]{3,0,2,1:T(8,128)(2,1)S(1)}, u32[]{:S(2)}, u32[]{:S(2)}) %all-to-all-start.3) | async-done | bytes 1671200 | tf_op jit(solution)/shard_map/all_to_all | solution.py:92
  464.2 2.1 copy.70
  466.2 2.7 reshape.212
  468.9 4.0 gather_fusion.2
  472.9 1.7 bitcast_reduce_fusion
  474.7 12.1 %reduce-scatter.4.cloned.1.call-done = bf16[16,768,192]{1,2,0:T(8,128)(2,1)} async-done(((bf16[16,768,384]{1,2,0:T(8,128)(2,1)}), bf16[16,768,192]{1,2,0:T(8,128)(2,1)}) %reduce-scatter.4.cloned.1.call-update) | async-done | bytes 4718608 | tf_op jit(solution)/shard_map/reduce_scatter | solution.py:119
  486.8 113.3 %reduce-scatter.6.cloned.1.call-done = bf16[16,768,192]{1,2,0:T(8,128)(2,1)} async-done(((bf16[16,768,384]{1,2,0:T(8,128)(2,1)}), bf16[16,768,192]{1,2,0:T(8,128)(2,1)}) %reduce-scatter.6.cloned.1.call-update) | async-done | bytes 4718608 | tf_op jit(solution)/shard_map/reduce_scatter | solution.py:122
  600.1 113.3 %reduce-scatter.8.cloned.1.call-done = bf16[16,192,768]{2,1,0:T(8,128)(2,1)} async-done(((bf16[16,384,768]{2,1,0:T(8,128)(2,1)}), bf16[16,192,768]{2,1,0:T(8,128)(2,1)}) %reduce-scatter.8.cloned.1.call-update) | async-done | bytes 4718608 | tf_op jit(solution)/shard_map/reduce_scatter | solution.py:125
  (47 shorter events, 1.1 us)
Async XLA Ops:
  7.2 28.0 %copy-start = (bf16[128,768]{1,0:T(8,128)(2,1)S(1)}, bf16[128,768]{1,0:T(8,128)(2,1)}, u32[]{:S(2)}) copy-start(bf16[128,768]{1,0:T(8,128)(2,1)} %param.7) | copy-start | bytes 589828
  7.2 207.9 %all-gather.5.cloned.1.call-start = ((), (), s32[]{:S(2)}) async-start(), calls=%async_computation.9 | async-start | bytes 14155776 | tf_op jit(solution)/shard_map/all_gather | solution.py:60
  7.9 3.8 copy-start.7
  7.9 328.2 %all-gather.3.cloned.1.call-start = ((), (), s32[]{:S(2)}) async-start(), calls=%async_computation.8 | async-start | bytes 14155776 | tf_op jit(solution)/shard_map/all_gather | solution.py:61
  8.7 191.6 %collective-permute-start = (bf16[16,768,192]{1,2,0:T(8,128)(2,1)}, bf16[16,768,192]{1,2,0:T(8,128)(2,1)}, u32[]{:S(2)}, u32[]{:S(2)}) collective-permute-start(bf16[16,768,192]{1,2,0:T(8,128)(2,1)} %param.11), channel_id=1, source_target_pairs={{0,2},{2,0},{1,3},{3,1},{4,6},{6,4},{5,7},{7,5},{8,10},{10,8},{9,1... | collective-permute-start | bytes 14155784 | tf_op jit(solution)/shard_map/ppermute | solution.py:11
  39.9 10.3 %copy-start.2 = (bf16[128,768]{1,0:T(8,128)(2,1)S(1)}, bf16[128,768]{1,0:T(8,128)(2,1)}, u32[]{:S(2)}) copy-start(bf16[128,768]{1,0:T(8,128)(2,1)} %param.8) | copy-start | bytes 589828
  64.2 5.0 copy-start.3
  64.2 43.9 %all-to-all-start.2 = ((bf16[16,4,17,768]{3,0,2,1:T(8,128)(2,1)}), bf16[16,4,17,768]{3,0,2,1:T(8,128)(2,1)}, u32[]{:S(2)}, u32[]{:S(2)}) async-start(bf16[16,4,17,768]{3,0,2,1:T(8,128)(2,1)} %copy.64), calls=%async_computation.2 | async-start | bytes 3342336 | tf_op jit(solution)/shard_map/all_to_all | solution.py:54
  108.1 114.9 %all-to-all-start.1 = ((bf16[16,4,17,768]{3,0,2,1:T(8,128)(2,1)}), bf16[16,4,17,768]{3,0,2,1:T(8,128)(2,1)S(1)}, u32[]{:S(2)}, u32[]{:S(2)}) async-start(bf16[16,4,17,768]{3,0,2,1:T(8,128)(2,1)} %copy.62), calls=%async_computation.1 | async-start | bytes 3342336 | tf_op jit(solution)/shard_map/all_to_all | solution.py:55
  111.7 254.5 %all-reduce.3.cloned.1.call-start = ((), (), s32[]{:S(2)}) async-start(), calls=%async_computation.13 | async-start | bytes 5308416 | tf_op jit(solution)/shard_map/psum | solution.py:80
  343.5 0.7 copy-start.8
  343.5 143.2 %reduce-scatter.4.cloned.1.call-start = ((), (), s32[]{:S(2)}) async-start(), calls=%async_computation.10 | async-start | bytes 14155776 | tf_op jit(solution)/shard_map/reduce_scatter | solution.py:119
  374.9 1.2 copy-start.4
  374.9 225.2 %reduce-scatter.6.cloned.1.call-start = ((), (), s32[]{:S(2)}) async-start(), calls=%async_computation.11 | async-start | bytes 14155776 | tf_op jit(solution)/shard_map/reduce_scatter | solution.py:122
  384.5 328.9 %reduce-scatter.8.cloned.1.call-start = ((), (), s32[]{:S(2)}) async-start(), calls=%async_computation.12 | async-start | bytes 14155776 | tf_op jit(solution)/shard_map/reduce_scatter | solution.py:125
  392.9 1.2 copy-start.5
  396.8 23.1 %all-to-all-start.4 = ((bf16[4,2,136]{2,1,0:T(2,128)(2,1)}), bf16[4,2,136]{2,1,0:T(2,128)(2,1)S(1)}, u32[]{:S(2)}, u32[]{:S(2)}) async-start(bf16[4,2,136]{2,1,0:T(2,128)(2,1)} %reshape.283), calls=%async_computation.4 | async-start | bytes 8192 | tf_op jit(solution)/shard_map/all_to_all | solution.py:99
  401.7 6.2 copy-start.6
  419.9 44.3 %all-to-all-start.3 = ((bf16[16,4,17,768]{3,0,2,1:T(8,128)(2,1)}), bf16[16,4,17,768]{3,0,2,1:T(8,128)(2,1)S(1)}, u32[]{:S(2)}, u32[]{:S(2)}) async-start(bf16[16,4,17,768]{3,0,2,1:T(8,128)(2,1)} %bitcast.6), calls=%async_computation.3 | async-start | bytes 3342336 | tf_op jit(solution)/shard_map/all_to_all | solution.py:92
  468.9 244.5 %copy-start.1 = (bf16[128,768]{1,0:T(8,128)(2,1)S(1)}, bf16[128,768]{1,0:T(8,128)(2,1)}, u32[]{:S(2)}) copy-start(bf16[128,768]{1,0:T(8,128)(2,1)} %param.7) | copy-start | bytes 589828
Sparse Core Ops, SparseCore 0:
  9.6 205.4 all-gather.4
  216.6 119.4 all-gather.2
  343.7 22.4 all-reduce.2
  375.1 111.6 reduce-scatter.3
  489.5 110.5 reduce-scatter.5
  602.8 110.5 reduce-scatter.7
